TPU v7x, 32 devices: a whole 2x2x4 slice. The times are simulated.
32 devices in a mesh: expert: 8 (over z, x), hidden: 4 (over y, core).
Axes of the slice: x: 2, y: 2, z: 4, core: 2. Of those that a mesh axis runs over, the one named last changes fastest.
Arguments:
- tokens: bfloat16 [768, 4096], P('expert', 'hidden'), may hold values from -6 to 6
- gate_weight: bfloat16 [16, 4096, 1536], P('expert', None, 'hidden'), may hold values from -0.09375 to 0.09375
- up_weight: bfloat16 [16, 4096, 1536], P('expert', None, 'hidden'), may hold values from -0.09375 to 0.09375
- down_weight: bfloat16 [16, 1536, 4096], P('expert', 'hidden'), may hold values from -0.15625 to 0.15625
- swap_slot: int32 [8], replicated, may hold values from 0 to 1
- expert_ids: int32 [768, 8], P('expert'), may hold values from 0 to 15, as said below
- gate_fixed: int32 [768, 8], P('expert'), may hold values from 1 to 65535
Outputs:
- moe_out: bfloat16 [768, 4096], P('expert', 'hidden')
Inputs may be any that keep to these rules, and one draw needn't show every extreme that they name: `expert_ids`: each row names 8 ids on 8 different indices of the expert axis (index = id // 2). In the 96 rows of each index of the expert axis, every index is named exactly 96 times.
All inputs are finite; a program needn't handle non-finite values.
Results may differ from a plain program's by a relative error of at most 0.012.
Values may be sent and summed in bfloat16 or wider, within the bound.
A program may use at most 192 MiB of HBM per device.

v0:
```python
import jax
import jax.numpy as jnp
from jax import lax
from jax.sharding import PartitionSpec as P


def slot_weights(expert_ids, gate_fixed, swap_slot, slots_here):
    axis_count = lax.axis_size("expert")
    me = lax.axis_index("expert")
    scores = gate_fixed.astype(jnp.float32)
    gate_norm = scores / jnp.sum(scores, axis=1, keepdims=True)
    home = expert_ids // slots_here
    slot = expert_ids % slots_here
    onehot = home[:, :, None] == jnp.arange(axis_count, dtype=jnp.int32)
    own_swap = jnp.sum(jnp.where(onehot, swap_slot, 0), axis=2)
    other_swap = jnp.sum(jnp.where(onehot, jnp.roll(swap_slot, -(axis_count // 2)), 0), axis=2)
    other = (home + axis_count // 2) % axis_count
    source = jnp.where(slot == own_swap, other * slots_here + other_swap, expert_ids)
    mine = me * slots_here + jnp.arange(slots_here, dtype=jnp.int32)
    return jnp.sum(jnp.where(source[:, :, None] == mine, gate_norm[:, :, None], 0.0), axis=1)


def per_device(tokens, gate_weight, up_weight, down_weight, swap_slot, expert_ids, gate_fixed):
    slots_here = gate_weight.shape[0]
    ids_all = lax.all_gather(expert_ids, "expert", axis=0, tiled=True)
    gates_all = lax.all_gather(gate_fixed, "expert", axis=0, tiled=True)
    weight = slot_weights(ids_all, gates_all, swap_slot, slots_here)
    rows = lax.all_gather(tokens, "hidden", axis=1, tiled=True)
    rows = lax.all_gather(rows, "expert", axis=0, tiled=True)
    total = None
    for s in range(slots_here):
        gate_out = jnp.dot(rows, gate_weight[s], preferred_element_type=jnp.float32)
        up_out = jnp.dot(rows, up_weight[s], preferred_element_type=jnp.float32)
        hidden = (jax.nn.silu(gate_out) * up_out * weight[:, s : s + 1]).astype(jnp.bfloat16)
        out = jnp.dot(hidden, down_weight[s], preferred_element_type=jnp.float32)
        total = out if total is None else total + out
    total = total.astype(jnp.bfloat16)
    part = lax.psum_scatter(total, "expert", scatter_dimension=0, tiled=True)
    return lax.psum_scatter(part, "hidden", scatter_dimension=1, tiled=True)


def solution(mesh):
    in_specs = (
        P("expert", "hidden"),
        P("expert", None, "hidden"),
        P("expert", None, "hidden"),
        P("expert", "hidden", None),
        P(),
        P("expert", None),
        P("expert", None),
    )
    return jax.shard_map(
        per_device, mesh=mesh, in_specs=in_specs, out_specs=P("expert", "hidden"), check_vma=False
    )
```

profile of v0, /device:TPU:0, one launch (start us, length us, event | category | flops | bytes accessed | tf_op | source)
XLA Modules:
  0.0 301.3 jit_solution(4140914008804489191)
XLA Ops:
  6.5 0.0 all-gather.4.cloned.1.call-start
  6.5 11.7 %all_gather.12 = bf16[96,4096]{1,0:T(8,128)(2,1)} all-gather(bf16[96,1024]{1,0:T(8,128)(2,1)} %param.7), channel_id=1, replica_groups=mesh['expert'=8,'hidden'=4] {'hidden'}, dimensions={1}, use_global_device_ids=true | all-gather | bytes 983040 | tf_op jit(solution)/shard_map/all_gather | solution.py:28
  18.2 0.0 all-gather.4.cloned.1.call-update
  18.3 0.0 reduce-scatter.3.cloned.1.call-start
  18.3 31.5 %all-gather.1 = s32[8,96,8]{1,2,0:T(8,128)S(1)} all-gather(s32[1,96,8]{1,2,0:T(8,128)} %bitcast.44), channel_id=1, replica_groups=mesh['expert'=8,'hidden'=4] {'expert'}, dimensions={0}, use_global_device_ids=true | all-gather | bytes 27648 | tf_op jit(solution)/shard_map/all_gather | solution.py:26
  49.8 0.1 reshape.12
  49.9 0.1 reshape.13
  50.0 30.9 %all-gather = s32[8,96,8]{1,2,0:T(8,128)S(1)} all-gather(s32[1,96,8]{1,2,0:T(8,128)} %bitcast.45), channel_id=1, replica_groups=mesh['expert'=8,'hidden'=4] {'expert'}, dimensions={0}, use_global_device_ids=true | all-gather | bytes 27648 | tf_op jit(solution)/shard_map/all_gather | solution.py:25
  80.9 0.1 reshape.9
  81.0 0.8 fusion.42
  81.8 0.1 pad_add_fusion
  81.9 0.8 select_reduce_fusion.1
  82.8 0.1 select_reduce_fusion.2
  82.9 35.3 %all-gather.4.cloned.1.call-done = bf16[768,4096]{1,0:T(8,128)(2,1)} async-done(((bf16[96,4096]{1,0:T(8,128)(2,1)}), bf16[768,4096]{1,0:T(8,128)(2,1)}) %all-gather.4.cloned.1.call-update) | async-done | bytes 6291472 | tf_op jit(solution)/shard_map/all_gather | solution.py:29
  118.2 0.0 copy-start
  118.2 0.0 slice-start
  118.2 0.0 slice-start.2
  118.2 6.6 %fusion.9 = f32[768,384]{1,0:T(8,128)S(1)} fusion(bf16[768,4096]{1,0:T(8,128)(2,1)} %all-gather.4.cloned.1.call-done, bf16[2,4096,384]{2,1,0:T(8,128)(2,1)} %param.8), kind=kOutput, calls=%fused_computation.10 | convolution fusion | flops 2415919104 | bytes 10616832 | tf_op jit(solution)/shard_map/dot_general | solution.py:32
  124.8 0.0 copy-done
  124.8 0.0 slice-start.1
  124.8 0.0 slice-start.3
  124.8 5.8 %fusion.29 = bf16[768,384]{1,0:T(8,128)(2,1)S(1)} fusion(bf16[768,4096]{1,0:T(8,128)(2,1)S(1)} %copy-done, bf16[2,4096,384]{2,1,0:T(8,128)(2,1)} %param.9, f32[768,384]{1,0:T(8,128)S(1)} %fusion.9, f32[768]{0:T(1024)S(1)} %get-tuple-element.8), kind=kOutput, calls=%fused_computation.22 | convolution fusion | flops 2417983488 | bytes 11209728 | tf_op jit(solution)/shard_map/dot_general | solution.py:33
  130.6 0.0 slice-done
  130.6 0.0 slice-done.1
  130.7 0.0 slice-start.4
  130.7 3.4 %fusion.5 = f32[768,4096]{1,0:T(8,128)S(1)} fusion(bf16[768,384]{1,0:T(8,128)(2,1)S(1)} %fusion.29, bf16[2,384,4096]{2,1,0:T(8,128)(2,1)S(1)} %bitcast.43), kind=kOutput, calls=%fused_computation.6 | convolution fusion | flops 2415919104 | bytes 16318464 | tf_op jit(solution)/shard_map/dot_general | solution.py:35
  134.1 0.0 slice-done.2
  134.1 0.0 slice-done.3
  134.1 0.0 slice-start.5
  134.2 5.7 %fusion.3 = f32[768,384]{1,0:T(8,128)S(1)} fusion(bf16[768,4096]{1,0:T(8,128)(2,1)} %all-gather.4.cloned.1.call-done, bf16[2,4096,384]{2,1,0:T(8,128)(2,1)S(1)} %bitcast.47), kind=kOutput, calls=%fused_computation.4 | convolution fusion | flops 2415919104 | bytes 10616832 | tf_op jit(solution)/shard_map/dot_general | solution.py:32
  139.8 0.0 slice-done.4
  139.9 0.0 slice-done.5
  139.9 6.3 %fusion.32 = bf16[768,384]{1,0:T(8,128)(2,1)S(1)} fusion(bf16[768,4096]{1,0:T(8,128)(2,1)} %all-gather.4.cloned.1.call-done, bf16[2,4096,384]{2,1,0:T(8,128)(2,1)S(1)} %bitcast.49, f32[768,384]{1,0:T(8,128)S(1)} %fusion.3, f32[768]{0:T(1024)S(1)} %get-tuple-element.7), kind=kOutput, calls=%fused_computation.23 | convolution fusion | flops 2417983488 | bytes 11210752 | tf_op jit(solution)/shard_map/dot_general | solution.py:33
  146.2 7.3 %add_convert_fusion = bf16[768,4096]{1,0:T(8,128)(2,1)} fusion(f32[768,4096]{1,0:T(8,128)S(1)} %fusion.5, bf16[768,384]{1,0:T(8,128)(2,1)S(1)} %fusion.32, bf16[2,384,4096]{2,1,0:T(8,128)(2,1)} %param.10), kind=kOutput, calls=%fused_computation | convolution fusion | flops 2422210560 | bytes 22609920 | tf_op jit(solution)/shard_map/dot_general | solution.py:35
  153.5 0.0 reduce-scatter.3.cloned.1.call-update
  153.5 0.0 reduce-scatter.5.cloned.1.call-start
  153.6 116.3 %reduce-scatter.3.cloned.1.call-done = bf16[96,4096]{1,0:T(8,128)(2,1)} async-done(((bf16[768,4096]{1,0:T(8,128)(2,1)}), bf16[96,4096]{1,0:T(8,128)(2,1)}) %reduce-scatter.3.cloned.1.call-update) | async-done | bytes 786448 | tf_op jit(solution)/shard_map/reduce_scatter | solution.py:38
  269.9 0.0 reduce-scatter.5.cloned.1.call-update
  269.9 24.9 %reduce-scatter.5.cloned.1.call-done = bf16[96,1024]{1,0:T(8,128)(2,1)} async-done(((bf16[96,4096]{1,0:T(8,128)(2,1)}), bf16[96,1024]{1,0:T(8,128)(2,1)}) %reduce-scatter.5.cloned.1.call-update) | async-done | bytes 196624 | tf_op jit(solution)/shard_map/reduce_scatter | solution.py:39
  (12 shorter events, 0.1 us)
Async XLA Ops:
  6.5 111.7 %all-gather.4.cloned.1.call-start = ((), (), s32[]{:S(2)}) async-start(), calls=%async_computation.2 | async-start | bytes 7077888 | tf_op jit(solution)/shard_map/all_gather | solution.py:29
  18.3 251.6 %reduce-scatter.3.cloned.1.call-start = ((), (), s32[]{:S(2)}) async-start(), calls=%async_computation.3 | async-start | bytes 7077888 | tf_op jit(solution)/shard_map/reduce_scatter | solution.py:38
  118.2 6.6 %copy-start = (bf16[768,4096]{1,0:T(8,128)(2,1)S(1)}, bf16[768,4096]{1,0:T(8,128)(2,1)}, u32[]{:S(2)}) copy-start(bf16[768,4096]{1,0:T(8,128)(2,1)} %all-gather.4.cloned.1.call-done) | copy-start | bytes 18874372
  118.2 12.4 %slice-start = ((s8[6291456]{0:T(1024)(128)(4,1)}), s8[4194304]{0:T(1024)(128)(4,1)S(1)}, s32[]{:S(2)}) async-start(s8[6291456]{0:T(1024)(128)(4,1)} %bitcast.42), calls=%async_computation.5 | async-start | bytes 8388608
  118.2 15.9 %slice-start.2 = ((s8[6291456]{0:T(1024)(128)(4,1)}), s8[4194304]{0:T(1024)(128)(4,1)S(1)}, s32[]{:S(2)}) async-start(s8[6291456]{0:T(1024)(128)(4,1)} %bitcast.46), calls=%async_computation.7 | async-start | bytes 8388608
  124.8 5.8 %slice-start.1 = ((s8[6291456]{0:T(1024)(128)(4,1)}), s8[2097152]{0:T(1024)(128)(4,1)S(1)}, s32[]{:S(2)}) async-start(s8[6291456]{0:T(1024)(128)(4,1)} %bitcast.42), calls=%async_computation.6 | async-start | bytes 4194304
  124.8 9.3 %slice-start.3 = ((s8[6291456]{0:T(1024)(128)(4,1)}), s8[2097152]{0:T(1024)(128)(4,1)S(1)}, s32[]{:S(2)}) async-start(s8[6291456]{0:T(1024)(128)(4,1)} %bitcast.46), calls=%async_computation.8 | async-start | bytes 4194304
  130.7 9.2 %slice-start.4 = ((s8[6291456]{0:T(1024)(128)(4,1)}), s8[2097152]{0:T(1024)(128)(4,1)S(1)}, s32[]{:S(2)}) async-start(s8[6291456]{0:T(1024)(128)(4,1)} %bitcast.48), calls=%async_computation.9 | async-start | bytes 4194304
  134.1 5.7 %slice-start.5 = ((s8[6291456]{0:T(1024)(128)(4,1)}), s8[4194304]{0:T(1024)(128)(4,1)S(1)}, s32[]{:S(2)}) async-start(s8[6291456]{0:T(1024)(128)(4,1)} %bitcast.48), calls=%async_computation.10 | async-start | bytes 8388608
  153.5 141.3 %reduce-scatter.5.cloned.1.call-start = ((), (), s32[]{:S(2)}) async-start(), calls=%async_computation.4 | async-start | bytes 983040 | tf_op jit(solution)/shard_map/reduce_scatter | solution.py:39
Sparse Core Ops, SparseCore 0:
  18.4 99.7 all-gather.3
  153.6 116.1 reduce-scatter.2
  272.4 22.3 reduce-scatter.4
where the time goes:
time: 302 us; the launch traced here: 301 us
  waiting for transfers between devices  177 us (59%)
  blocking collectives  74.1 us (25%)
  matrix products  35.1 us (12%)
  between operations  13.3 us (4%)
    reduce_scatter x1, waiting for transfers between devices, per_device(): part = lax.psum_scatter(total, 'expert', scatter_dimension=0, tiled=True)  116 us
    all_gather x1, waiting for transfers between devices, per_device(): rows = lax.all_gather(rows, 'expert', axis=0, tiled=True)  35.3 us
    all_gather x1, blocking collectives, per_device(): gates_all = lax.all_gather(gate_fixed, 'expert', axis=0, tiled=True)  31.5 us
    all_gather x1, blocking collectives, per_device(): ids_all = lax.all_gather(expert_ids, 'expert', axis=0, tiled=True)  30.9 us
    reduce_scatter x1, waiting for transfers between devices, per_device(): return lax.psum_scatter(part, 'hidden', scatter_dimension=1, tiled=True)  24.9 us
    dot_general x2, matrix products, per_device(): gate_out = jnp.dot(rows, gate_weight[s], preferred_element_type=jnp.float32)  12.2 us
    dot_general x2, matrix products, per_device(): up_out = jnp.dot(rows, up_weight[s], preferred_element_type=jnp.float32)  12.1 us
    all_gather x1, blocking collectives, per_device(): rows = lax.all_gather(tokens, 'hidden', axis=1, tiled=True)  11.7 us
  transfers between devices with their start and end apart: 3, of which 3 were waited for; matrix products, arithmetic and copies ran while one was open for 1% of the time, Pallas kernels for 0%

commit v1 on v0

--- a/solution.py
+++ b/solution.py
@@ -26,7 +26,24 @@
     gates_all = lax.all_gather(gate_fixed, "expert", axis=0, tiled=True)
     weight = slot_weights(ids_all, gates_all, swap_slot, slots_here)
     rows = lax.all_gather(tokens, "hidden", axis=1, tiled=True)
-    rows = lax.all_gather(rows, "expert", axis=0, tiled=True)
+    size, index, span = (lax.axis_size("expert"), lax.axis_index("expert"), rows.shape[0])
+    right = [(i, (i + 1) % size) for i in range(size)]
+    backward = [(i, (i - 1) % size) for i in range(size)]
+    result = jnp.zeros((*rows.shape[:0], size * span, *rows.shape[0 + 1 :]), rows.dtype)
+    result = lax.dynamic_update_slice_in_dim(result, rows, index * span, axis=0)
+    from_left = from_right = rows
+    halfway = size // 2
+    for step in range(1, halfway + 1):
+        from_left = lax.ppermute(from_left, "expert", right)
+        result = lax.dynamic_update_slice_in_dim(
+            result, from_left, (index - step) % size * span, axis=0
+        )
+        if step < size - halfway:
+            from_right = lax.ppermute(from_right, "expert", backward)
+            result = lax.dynamic_update_slice_in_dim(
+                result, from_right, (index + step) % size * span, axis=0
+            )
+    rows = result
     total = None
     for s in range(slots_here):
         gate_out = jnp.dot(rows, gate_weight[s], preferred_element_type=jnp.float32)

time: 302 us -> 367 us (1.22)
  starting transfers between devices: 0.09 us -> 27.6 us
  waiting for transfers between devices: 177 us -> 200 us
  blocking collectives: 74.1 us -> 97 us
  matrix products: 35.1 us -> 24.8 us
    ppermute x0 -> x7, waiting for transfers between devices: none -> 58.4 us  [the longest x4 38.7 us: per_device(): from_left = lax.ppermute(from_left, 'expert', right)]
    all_gather x1 -> x0, waiting for transfers between devices: 35.3 us -> none  [per_device(): rows = lax.all_gather(rows, 'expert', axis=0, tiled=True)]
    ppermute x0 -> x7, starting transfers between devices: none -> 27.6 us  [the longest x3 25.1 us: per_device(): from_right = lax.ppermute(from_right, 'expert', backward)]
    all_gather x1, blocking collectives: 31.5 us -> 56.1 us  [per_device(): gates_all = lax.all_gather(gate_fixed, 'expert', axis=0, tiled=True)]
    dot_general x2, matrix products: 12.2 us -> 6.85 us  [per_device(): gate_out = jnp.dot(rows, gate_weight[s], preferred_element_type=jnp.float32)]
    dot_general x2, matrix products: 12.1 us -> 6.85 us  [per_device(): up_out = jnp.dot(rows, up_weight[s], preferred_element_type=jnp.float32)]
  transfers between devices with their start and end apart: 3 -> 9, of which waited for: 3 -> 5; matrix products, arithmetic and copies ran while one was open for 1% -> 1% of each run, Pallas kernels for 0% -> 0%
where the time goes in v1:
time: 367 us
  waiting for transfers between devices  200 us (54%)
  blocking collectives  97 us (26%)
  starting transfers between devices  27.6 us (8%)
  matrix products  24.8 us (7%)
  between operations  13.7 us (4%)
    reduce_scatter x1, waiting for transfers between devices, per_device(): part = lax.psum_scatter(total, 'expert', scatter_dimension=0, tiled=True)  117 us
    all_gather x1, blocking collectives, per_device(): gates_all = lax.all_gather(gate_fixed, 'expert', axis=0, tiled=True)  56.1 us
    ppermute x4, waiting for transfers between devices, per_device(): from_left = lax.ppermute(from_left, 'expert', right)  38.7 us
    all_gather x1, blocking collectives, per_device(): ids_all = lax.all_gather(expert_ids, 'expert', axis=0, tiled=True)  30.6 us
    ppermute x3, starting transfers between devices, per_device(): from_right = lax.ppermute(from_right, 'expert', backward)  25.1 us
    reduce_scatter x1, waiting for transfers between devices, per_device(): return lax.psum_scatter(part, 'hidden', scatter_dimension=1, tiled=True)  24.9 us
    ppermute x3, waiting for transfers between devices, per_device(): from_right = lax.ppermute(from_right, 'expert', backward)  19.7 us
    dot_general x2, matrix products, per_device(): out = jnp.dot(hidden, down_weight[s], preferred_element_type=jnp.float32)  11.1 us
  transfers between devices with their start and end apart: 9, of which 5 were waited for; matrix products, arithmetic and copies ran while one was open for 1% of the time, Pallas kernels for 0%

profile of v1, /device:TPU:0, one launch (start us, length us, event | category | flops | bytes accessed | tf_op | source)
XLA Modules:
  0.0 367.0 jit_solution(16371602885482716476)
XLA Ops:
  6.5 10.3 %all_gather.9 = bf16[96,4096]{1,0:T(8,128)(2,1)S(1)} all-gather(bf16[96,1024]{1,0:T(8,128)(2,1)} %param.7), channel_id=1, replica_groups=mesh['expert'=8,'hidden'=4] {'hidden'}, dimensions={1}, use_global_device_ids=true | all-gather | bytes 983040 | tf_op jit(solution)/shard_map/all_gather | solution.py:28
  16.8 4.5 %collective-permute-start.1 = (bf16[96,4096]{1,0:T(8,128)(2,1)S(1)}, bf16[96,4096]{1,0:T(8,128)(2,1)S(1)}, u32[]{:S(2)}, u32[]{:S(2)}) collective-permute-start(bf16[96,4096]{1,0:T(8,128)(2,1)S(1)} %all_gather.9), channel_id=1, source_target_pairs={{0,28},{4,0},{8,4},{12,8},{16,12},{20,16},{24,20},{28,24},{1,29},{... | collective-permute-start | bytes 2359304 | tf_op jit(solution)/shard_map/ppermute | solution.py:42
  21.3 0.0 collective-permute-start
  21.3 56.1 %all-gather.1 = s32[8,96,8]{1,2,0:T(8,128)S(1)} all-gather(s32[1,96,8]{1,2,0:T(8,128)} %bitcast.30), channel_id=1, replica_groups=mesh['expert'=8,'hidden'=4] {'expert'}, dimensions={0}, use_global_device_ids=true | all-gather | bytes 27648 | tf_op jit(solution)/shard_map/all_gather | solution.py:26
  77.5 0.8 fusion.30
  78.3 0.1 reshape.12
  78.4 0.1 reshape.13
  78.5 30.6 %all-gather = s32[8,96,8]{1,2,0:T(8,128)S(1)} all-gather(s32[1,96,8]{1,2,0:T(8,128)} %bitcast.31), channel_id=1, replica_groups=mesh['expert'=8,'hidden'=4] {'expert'}, dimensions={0}, use_global_device_ids=true | all-gather | bytes 27648 | tf_op jit(solution)/shard_map/all_gather | solution.py:25
  109.1 0.1 reshape.9
  109.2 0.1 pad_add_fusion
  109.3 0.8 select_reduce_fusion.1
  110.2 0.1 select_reduce_fusion.2
  110.4 0.0 slice-start.2
  110.4 0.8 broadcast_in_dim.33
  111.1 0.1 constant_dynamic-update-slice_fusion.7
  111.2 0.0 collective-permute-done.1
  111.2 8.2 %collective-permute-start.3 = (bf16[96,4096]{1,0:T(8,128)(2,1)S(1)}, bf16[96,4096]{1,0:T(8,128)(2,1)S(1)}, u32[]{:S(2)}, u32[]{:S(2)}) collective-permute-start(bf16[96,4096]{1,0:T(8,128)(2,1)S(1)} %collective-permute-done.1), channel_id=1, source_target_pairs={{0,28},{4,0},{8,4},{12,8},{16,12},{20,16},{24,20},{28,24},{1,29},{... | collective-permute-start | bytes 2359304 | tf_op jit(solution)/shard_map/ppermute | solution.py:42
  119.4 0.0 collective-permute-done
  119.4 0.0 collective-permute-start.2
  119.4 0.1 constant_dynamic-update-slice_fusion.6
  119.5 0.0 slice-start.3
  119.5 0.1 constant_dynamic-update-slice_fusion.5
  119.6 19.7 %collective-permute-done.3 = bf16[96,4096]{1,0:T(8,128)(2,1)S(1)} collective-permute-done((bf16[96,4096]{1,0:T(8,128)(2,1)S(1)}, bf16[96,4096]{1,0:T(8,128)(2,1)S(1)}, u32[]{:S(2)}, u32[]{:S(2)}) %collective-permute-start.3) | collective-permute-done | bytes 786464 | tf_op jit(solution)/shard_map/ppermute | solution.py:42
  139.3 12.4 %collective-permute-start.5 = (bf16[96,4096]{1,0:T(8,128)(2,1)S(1)}, bf16[96,4096]{1,0:T(8,128)(2,1)S(1)}, u32[]{:S(2)}, u32[]{:S(2)}) collective-permute-start(bf16[96,4096]{1,0:T(8,128)(2,1)S(1)} %collective-permute-done.3), channel_id=1, source_target_pairs={{0,28},{4,0},{8,4},{12,8},{16,12},{20,16},{24,20},{28,24},{1,29},{... | collective-permute-start | bytes 2359304 | tf_op jit(solution)/shard_map/ppermute | solution.py:42
  151.8 0.1 constant_dynamic-update-slice_fusion.4
  151.8 0.1 constant_dynamic-update-slice_fusion.3
  151.9 25.5 %collective-permute-done.4 = bf16[96,4096]{1,0:T(8,128)(2,1)S(1)} collective-permute-done((bf16[96,4096]{1,0:T(8,128)(2,1)S(1)}, bf16[96,4096]{1,0:T(8,128)(2,1)S(1)}, u32[]{:S(2)}, u32[]{:S(2)}) %collective-permute-start.4) | collective-permute-done | bytes 786464 | tf_op jit(solution)/shard_map/ppermute | solution.py:37
  177.4 2.5 collective-permute-start.6
  179.9 0.1 constant_dynamic-update-slice_fusion.2
  179.9 0.0 collective-permute-done.5
  179.9 0.1 constant_dynamic-update-slice_fusion.1
  180.0 13.2 %collective-permute-done.6 = bf16[96,4096]{1,0:T(8,128)(2,1)S(1)} collective-permute-done((bf16[96,4096]{1,0:T(8,128)(2,1)S(1)}, bf16[96,4096]{1,0:T(8,128)(2,1)S(1)}, u32[]{:S(2)}, u32[]{:S(2)}) %collective-permute-start.6) | collective-permute-done | bytes 786464 | tf_op jit(solution)/shard_map/ppermute | solution.py:37
  193.2 0.1 constant_dynamic-update-slice_fusion
  193.3 0.0 slice-start.4
  193.3 3.4 fusion.1
  196.8 0.0 slice-start.5
  196.8 3.4 fusion.7
  200.2 0.0 slice-start
  200.2 3.4 fusion.3
  203.7 0.0 slice-start.1
  203.7 3.4 fusion.9
  207.1 3.5 fusion.5
  210.7 7.6 %add_convert_fusion = bf16[768,4096]{1,0:T(8,128)(2,1)} fusion(f32[768,4096]{1,0:T(8,128)S(1)} %fusion.5, bf16[2,384,4096]{2,1,0:T(8,128)(2,1)} %param.10, f32[768,384]{1,0:T(8,128)S(1)} %fusion.1, f32[768,384]{1,0:T(8,128)S(1)} %fusion.3, f32[768]{0:T(1024)S(1)} %get-tuple-element.7), kind=kOutput, calls=%fused_computation | convolution fusion | flops 2424274944 | bytes 24382464 | tf_op jit(solution)/shard_map/dot_general | solution.py:52
  218.3 0.0 reduce-scatter.3.cloned.1.call-update
  218.3 0.0 reduce-scatter.5.cloned.1.call-start
  218.4 116.9 %reduce-scatter.3.cloned.1.call-done = bf16[96,4096]{1,0:T(8,128)(2,1)} async-done(((bf16[768,4096]{1,0:T(8,128)(2,1)}), bf16[96,4096]{1,0:T(8,128)(2,1)}) %reduce-scatter.3.cloned.1.call-update) | async-done | bytes 786448 | tf_op jit(solution)/shard_map/reduce_scatter | solution.py:55
  335.2 0.0 reduce-scatter.5.cloned.1.call-update
  335.2 24.9 %reduce-scatter.5.cloned.1.call-done = bf16[96,1024]{1,0:T(8,128)(2,1)} async-done(((bf16[96,4096]{1,0:T(8,128)(2,1)}), bf16[96,1024]{1,0:T(8,128)(2,1)}) %reduce-scatter.5.cloned.1.call-update) | async-done | bytes 196624 | tf_op jit(solution)/shard_map/reduce_scatter | solution.py:56
  (21 shorter events, 0.2 us)
Async XLA Ops:
  6.5 328.7 %reduce-scatter.3.cloned.1.call-start = ((), (), s32[]{:S(2)}) async-start(), calls=%async_computation.2 | async-start | bytes 7077888 | tf_op jit(solution)/shard_map/reduce_scatter | solution.py:55
  16.8 94.4 %collective-permute-start.1 = (bf16[96,4096]{1,0:T(8,128)(2,1)S(1)}, bf16[96,4096]{1,0:T(8,128)(2,1)S(1)}, u32[]{:S(2)}, u32[]{:S(2)}) collective-permute-start(bf16[96,4096]{1,0:T(8,128)(2,1)S(1)} %all_gather.9), channel_id=1, source_target_pairs={{0,28},{4,0},{8,4},{12,8},{16,12},{20,16},{24,20},{28,24},{1,29},{... | collective-permute-start | bytes 2359304 | tf_op jit(solution)/shard_map/ppermute | solution.py:42
  21.3 98.1 %collective-permute-start = (bf16[96,4096]{1,0:T(8,128)(2,1)S(1)}, bf16[96,4096]{1,0:T(8,128)(2,1)S(1)}, u32[]{:S(2)}, u32[]{:S(2)}) collective-permute-start(bf16[96,4096]{1,0:T(8,128)(2,1)S(1)} %all_gather.9), channel_id=1, source_target_pairs={{0,4},{4,8},{8,12},{12,16},{16,20},{20,24},{24,28},{28,0},{1,5},{5... | collective-permute-start | bytes 2359304 | tf_op jit(solution)/shard_map/ppermute | solution.py:37
  110.4 82.9 %slice-start.2 = ((s8[6291456]{0:T(1024)(128)(4,1)}), s8[2097152]{0:T(1024)(128)(4,1)S(1)}, s32[]{:S(2)}) async-start(s8[6291456]{0:T(1024)(128)(4,1)} %bitcast.32), calls=%async_computation.6 | async-start | bytes 4194304
  111.2 28.1 %collective-permute-start.3 = (bf16[96,4096]{1,0:T(8,128)(2,1)S(1)}, bf16[96,4096]{1,0:T(8,128)(2,1)S(1)}, u32[]{:S(2)}, u32[]{:S(2)}) collective-permute-start(bf16[96,4096]{1,0:T(8,128)(2,1)S(1)} %collective-permute-done.1), channel_id=1, source_target_pairs={{0,28},{4,0},{8,4},{12,8},{16,12},{20,16},{24,20},{28,24},{1,29},{... | collective-permute-start | bytes 2359304 | tf_op jit(solution)/shard_map/ppermute | solution.py:42
  119.4 32.3 %collective-permute-start.2 = (bf16[96,4096]{1,0:T(8,128)(2,1)S(1)}, bf16[96,4096]{1,0:T(8,128)(2,1)S(1)}, u32[]{:S(2)}, u32[]{:S(2)}) collective-permute-start(bf16[96,4096]{1,0:T(8,128)(2,1)S(1)} %collective-permute-done), channel_id=1, source_target_pairs={{0,4},{4,8},{8,12},{12,16},{16,20},{20,24},{24,28},{28,0},{1,5},{5... | collective-permute-start | bytes 2359304 | tf_op jit(solution)/shard_map/ppermute | solution.py:37
  119.5 73.8 %slice-start.3 = ((s8[6291456]{0:T(1024)(128)(4,1)}), s8[4194304]{0:T(1024)(128)(4,1)S(1)}, s32[]{:S(2)}) async-start(s8[6291456]{0:T(1024)(128)(4,1)} %bitcast.32), calls=%async_computation.7 | async-start | bytes 8388608
  139.3 40.6 %collective-permute-start.5 = (bf16[96,4096]{1,0:T(8,128)(2,1)S(1)}, bf16[96,4096]{1,0:T(8,128)(2,1)S(1)}, u32[]{:S(2)}, u32[]{:S(2)}) collective-permute-start(bf16[96,4096]{1,0:T(8,128)(2,1)S(1)} %collective-permute-done.3), channel_id=1, source_target_pairs={{0,28},{4,0},{8,4},{12,8},{16,12},{20,16},{24,20},{28,24},{1,29},{... | collective-permute-start | bytes 2359304 | tf_op jit(solution)/shard_map/ppermute | solution.py:42
  151.8 25.6 %collective-permute-start.4 = (bf16[96,4096]{1,0:T(8,128)(2,1)S(1)}, bf16[96,4096]{1,0:T(8,128)(2,1)S(1)}, u32[]{:S(2)}, u32[]{:S(2)}) collective-permute-start(bf16[96,4096]{1,0:T(8,128)(2,1)S(1)} %collective-permute-done.2), channel_id=1, source_target_pairs={{0,4},{4,8},{8,12},{12,16},{16,20},{20,24},{24,28},{28,0},{1,5},{5... | collective-permute-start | bytes 2359304 | tf_op jit(solution)/shard_map/ppermute | solution.py:37
  177.4 15.8 %collective-permute-start.6 = (bf16[96,4096]{1,0:T(8,128)(2,1)S(1)}, bf16[96,4096]{1,0:T(8,128)(2,1)S(1)}, u32[]{:S(2)}, u32[]{:S(2)}) collective-permute-start(bf16[96,4096]{1,0:T(8,128)(2,1)S(1)} %collective-permute-done.4), channel_id=1, source_target_pairs={{0,4},{4,8},{8,12},{12,16},{16,20},{20,24},{24,28},{28,0},{1,5},{5... | collective-permute-start | bytes 2359304 | tf_op jit(solution)/shard_map/ppermute | solution.py:37
  193.3 6.9 %slice-start.4 = ((s8[6291456]{0:T(1024)(128)(4,1)}), s8[4194304]{0:T(1024)(128)(4,1)S(1)}, s32[]{:S(2)}) async-start(s8[6291456]{0:T(1024)(128)(4,1)} %bitcast.34), calls=%async_computation.8 | async-start | bytes 8388608
  196.8 3.5 slice-start.5
  200.2 6.9 %slice-start = ((s8[6291456]{0:T(1024)(128)(4,1)}), s8[4194304]{0:T(1024)(128)(4,1)S(1)}, s32[]{:S(2)}) async-start(s8[6291456]{0:T(1024)(128)(4,1)} %bitcast.28), calls=%async_computation.4 | async-start | bytes 8388608
  203.7 3.5 slice-start.1
  218.3 141.9 %reduce-scatter.5.cloned.1.call-start = ((), (), s32[]{:S(2)}) async-start(), calls=%async_computation.3 | async-start | bytes 983040 | tf_op jit(solution)/shard_map/reduce_scatter | solution.py:56
Sparse Core Ops, SparseCore 0:
  218.4 116.7 reduce-scatter.2
  337.7 22.3 reduce-scatter.4
